TPU v7x, 256 devices: a whole 4x4x8 slice. The times are simulated.
256 devices in a mesh: fsdp: 128 (over x, z, y), tp: 2 (over core).
Axes of the slice: x: 4, y: 4, z: 8, core: 2. Of those that a mesh axis runs over, the one named last changes fastest.
Arguments:
- gate_gradient: bfloat16 [48, 524288], P(None, ('fsdp', 'tp')), may hold values from -40 to 40
- gate_velocity: float32 [48, 524288], P(None, ('fsdp', 'tp')), may hold values from -6 to 6
- rate_factor_gradient: bfloat16 [96, 196608], P(None, ('fsdp', 'tp')), may hold values from -40 to 40
- rate_factor_velocity: float32 [96, 196608], P(None, ('fsdp', 'tp')), may hold values from -6 to 6
- value_gradient: bfloat16 [48, 131072], P(None, ('fsdp', 'tp')), may hold values from -40 to 40
- value_velocity: float32 [48, 131072], P(None, ('fsdp', 'tp')), may hold values from -6 to 6
- vector_weights: float32 [933888], P(('fsdp', 'tp')), may hold values from -6 to 6
- vector_gradient: bfloat16 [933888], P(('fsdp', 'tp')), may hold values from -6 to 6
- vector_first_moment: float32 [933888], P(('fsdp', 'tp')), may hold values from -4 to 4
- vector_second_moment: float32 [933888], P(('fsdp', 'tp')), may hold values from 0.05 to 2
Outputs:
- update_gate: float32 [48, 524288], P(None, ('fsdp', 'tp'))
- update_lora: float32 [96, 196608], P(None, ('fsdp', 'tp'))
- update_value: float32 [48, 131072], P(None, ('fsdp', 'tp'))
- momentum_gate_out: float32 [48, 524288], P(None, ('fsdp', 'tp'))
- momentum_lora_out: float32 [96, 196608], P(None, ('fsdp', 'tp'))
- momentum_value_out: float32 [48, 131072], P(None, ('fsdp', 'tp'))
- vec_param_out: float32 [933888], P(('fsdp', 'tp'))
- vec_first_out: float32 [933888], P(('fsdp', 'tp'))
- vec_second_out: float32 [933888], P(('fsdp', 'tp'))
All inputs are finite; a program needn't handle non-finite values.
Results may differ from a plain program's by a relative error of at most 0.0032.
Values may be sent and summed in bfloat16 or wider, within the bound.
A program may use at most 64 MiB of HBM per device.

v0:
```python
import math

import jax
import jax.numpy as jnp
from jax import lax
from jax.sharding import PartitionSpec as P

MODEL_WIDTH = 2048
RG = 256
RATE_RANK = 96
RV = 64
NS_STEPS = 5


momentum_rate = 0.95
coef_linear = 3.4445
coef_gram = -4.775
coef_square = 2.0315
bias_first = 1.0 - 0.9**10
bias_second = 1.0 - 0.95**10
highest = lax.Precision.HIGHEST


def refresh_velocity(gradient, momentum_in):
    widened = gradient.astype(jnp.float32)
    renewed = momentum_rate * momentum_in + widened
    blended = (widened + momentum_rate * renewed).astype(jnp.bfloat16)
    return (renewed, blended)


def owner_slots(flat_rows, owners):
    matrix_count = flat_rows.shape[0]
    capacity = -(-matrix_count // owners)
    padded = jnp.pad(flat_rows, ((0, capacity * owners - matrix_count), (0, 0)))
    return padded.reshape(capacity, owners, flat_rows.shape[1])


def normalized(matrices):
    widened = matrices.astype(jnp.float32)
    frobenius = jnp.sqrt(jnp.sum(widened * widened, axis=(1, 2), keepdims=True))
    return widened / (frobenius + 1e-07)


def gram_terms(matrices):
    return jnp.einsum(
        "crd,csd->crs", matrices, matrices, preferred_element_type=jnp.float32, precision=highest
    )


def polish(matrices, gram_full):
    squared = jnp.einsum(
        "crs,cst->crt", gram_full, gram_full, preferred_element_type=jnp.float32, precision=highest
    )
    poly_full = coef_gram * gram_full + coef_square * squared
    applied = jnp.einsum(
        "crs,csd->crd", poly_full, matrices, preferred_element_type=jnp.float32, precision=highest
    )
    return coef_linear * matrices + applied


def adamw_shard(param_in, grad_in, first_in, second_in):
    widened = grad_in.astype(jnp.float32)
    first_moment_output = 0.9 * first_in + 0.1 * widened
    second_moment_output = 0.95 * second_in + 0.05 * widened * widened
    direction = (
        first_moment_output / bias_first / (jnp.sqrt(second_moment_output / bias_second) + 1e-08)
    )
    parameter_output = param_in - 0.05 * (direction + 0.1 * param_in)
    return (parameter_output, first_moment_output, second_moment_output)


def local(
    gate_gradient,
    gate_velocity,
    rate_factor_gradient,
    rate_factor_velocity,
    value_gradient,
    value_velocity,
    vector_weights,
    vector_gradient,
    vector_first_moment,
    vector_second_moment,
):
    owners = lax.axis_size("fsdp")
    pairs = lax.axis_size("tp")
    pair_lane = lax.axis_index("tp")
    gate_refreshed, gate_mixture = refresh_velocity(gate_gradient, gate_velocity)
    rate_factor_refreshed, rate_factor_mixture = refresh_velocity(
        rate_factor_gradient, rate_factor_velocity
    )
    value_refreshed, value_mixture = refresh_velocity(value_gradient, value_velocity)
    mixed_results = (gate_mixture, rate_factor_mixture, value_mixture)
    row_counts = (RG, RATE_RANK, RV)
    joined = (
        lax.all_gather(gate_mixture[:, None, :], "tp", axis=1, tiled=True),
        lax.all_gather(rate_factor_mixture[:, None, :], "tp", axis=1, tiled=True),
        lax.all_gather(value_mixture[:, None, :], "tp", axis=1, tiled=True),
    )
    slotted = tuple(
        (owner_slots(shard_rows.reshape(shard_rows.shape[0], -1), owners) for shard_rows in joined)
    )
    arrived = (
        lax.all_to_all(slotted[0], "fsdp", split_axis=1, concat_axis=1, tiled=True),
        lax.all_to_all(slotted[1], "fsdp", split_axis=1, concat_axis=1, tiled=True),
        lax.all_to_all(slotted[2], "fsdp", split_axis=1, concat_axis=1, tiled=True),
    )
    whole = tuple(
        (
            normalized(arrival.reshape(arrival.shape[0], row_total, MODEL_WIDTH))
            for arrival, row_total in zip(arrived, row_counts)
        )
    )
    parameter_output, first_moment_output, second_moment_output = adamw_shard(
        vector_weights, vector_gradient, vector_first_moment, vector_second_moment
    )
    current = whole
    for iteration in range(NS_STEPS):
        current = tuple((polish(matrices, gram_terms(matrices)) for matrices in current))
    outgoing = tuple(
        (
            lax.dynamic_index_in_dim(
                matrices.reshape(matrices.shape[0], owners, pairs, -1), pair_lane, 2, keepdims=False
            )
            for matrices in current
        )
    )
    returned = (
        lax.all_to_all(outgoing[0], "fsdp", split_axis=1, concat_axis=1, tiled=True),
        lax.all_to_all(outgoing[1], "fsdp", split_axis=1, concat_axis=1, tiled=True),
        lax.all_to_all(outgoing[2], "fsdp", split_axis=1, concat_axis=1, tiled=True),
    )
    scale_factor = math.sqrt(MODEL_WIDTH)
    updates = tuple(
        (
            landed.reshape(-1, landed.shape[2])[: source.shape[0]] * scale_factor
            for landed, source in zip(returned, mixed_results)
        )
    )
    return (
        updates[0],
        updates[1],
        updates[2],
        gate_refreshed,
        rate_factor_refreshed,
        value_refreshed,
        parameter_output,
        first_moment_output,
        second_moment_output,
    )


def solution(mesh):
    in_specs = (
        P(None, ("fsdp", "tp")),
        P(None, ("fsdp", "tp")),
        P(None, ("fsdp", "tp")),
        P(None, ("fsdp", "tp")),
        P(None, ("fsdp", "tp")),
        P(None, ("fsdp", "tp")),
        P(("fsdp", "tp")),
        P(("fsdp", "tp")),
        P(("fsdp", "tp")),
        P(("fsdp", "tp")),
    )
    out_specs = (
        P(None, ("fsdp", "tp")),
        P(None, ("fsdp", "tp")),
        P(None, ("fsdp", "tp")),
        P(None, ("fsdp", "tp")),
        P(None, ("fsdp", "tp")),
        P(None, ("fsdp", "tp")),
        P(("fsdp", "tp")),
        P(("fsdp", "tp")),
        P(("fsdp", "tp")),
    )
    return jax.shard_map(local, mesh=mesh, in_specs=in_specs, out_specs=out_specs, check_vma=False)
```

profile of v0, /device:TPU:32, one launch (start us, length us, event | category | flops | bytes accessed | tf_op | source)
XLA Modules:
  0.0 234.1 jit_solution(12493268743470985444)
XLA Ops:
  0.7 1.6 fusion.17
  2.3 1.9 all-gather.2
  5.1 2.1 reduce.20
  7.3 0.9 reshape.454
  8.2 15.0 %all-to-all-start.4 = ((bf16[128,2,512]{2,1,0:T(2,128)(2,1)}), bf16[128,2,512]{2,1,0:T(2,128)(2,1)S(1)}, u32[]{:S(2)}, u32[]{:S(2)}) async-start(bf16[128,2,512]{2,1,0:T(2,128)(2,1)} %reshape.454), calls=%async_computation.4 | async-start | bytes 524288 | tf_op jit(solution)/shard_map/all_to_all | solution.py:105
  23.2 0.8 fusion.15
  24.0 2.3 all-gather
  26.3 2.4 %copy.34 = bf16[1,128,4096]{2,0,1:T(2,128)(2,1)S(1)} copy(bf16[1,128,4096]{2,1,0:T(8,128)(2,1)S(1)} %pad_bitcast_fusion) | data formatting | bytes 2097152 | tf_op jit(solution)/shard_map/reshape | solution.py:35
  28.7 7.1 %reduce.18 = bf16[128,4096]{1,0:T(8,128)(2,1)S(1)} reduce(bf16[128,1,4096]{2,1,0:T(2,128)(2,1)S(1)} %bitcast.129, bf16[]{:T(256)} %broadcast.229), dimensions={1}, to_apply=%bitcast.126.reduce_sub_computation | reduce | bytes 2097154
  35.8 1.6 reshape.450
  38.2 2.4 %all-gather.1 = bf16[96,1536]{1,0:T(8,128)(2,1)S(1)} all-gather(bf16[96,768]{1,0:T(8,128)(2,1)S(1)} %get-tuple-element.20), channel_id=3, replica_groups=mesh['fsdp'=128,'tp'=2] {'tp'}, dimensions={1}, use_global_device_ids=true | all-gather | bytes 442368 | tf_op jit(solution)/shard_map/all_gather | solution.py:96
  41.2 3.0 %reduce.19 = bf16[128,1536]{1,0:T(8,128)(2,1)S(1)} reduce(bf16[128,1,1536]{2,1,0:T(2,128)(2,1)S(1)} %bitcast.130, bf16[]{:T(256)} %broadcast.229), dimensions={1}, to_apply=%bitcast.127.reduce_sub_computation | reduce | bytes 786434
  44.2 0.8 reshape.452
  45.1 13.8 %all-to-all-start.2 = ((bf16[128,2,768]{2,1,0:T(2,128)(2,1)}), bf16[128,2,768]{2,1,0:T(2,128)(2,1)S(1)}, u32[]{:S(2)}, u32[]{:S(2)}) async-start(bf16[128,2,768]{2,1,0:T(2,128)(2,1)} %reshape.452), calls=%async_computation.2 | async-start | bytes 786432 | tf_op jit(solution)/shard_map/all_to_all | solution.py:104
  59.1 1.7 multiply_reduce_fusion.5
  61.5 2.9 %fusion.22 = (f32[128,1024]{1,0:T(8,128)S(1)}, f32[128,1024]{1,0:T(8,128)S(1)}) fusion(f32[]{:T(128)S(6)} %add.208, bf16[128,1,1024]{2,1,0:T(2,128)(2,1)S(1)} %reshape.455), kind=kLoop, calls=%fused_computation.82 | loop fusion | flops 393216 | bytes 1310724 | tf_op jit(solution)/shard_map/div | solution.py:41
  71.9 0.9 dynamic-slice_bitcast_fusion.2
  72.9 2.9 %all-to-all-done.2 = bf16[128,2,768]{2,1,0:T(2,128)(2,1)S(1)} async-done(((bf16[128,2,768]{2,1,0:T(2,128)(2,1)}), bf16[128,2,768]{2,1,0:T(2,128)(2,1)S(1)}, u32[]{:S(2)}, u32[]{:S(2)}) %all-to-all-start.2) | async-done | bytes 393248 | tf_op jit(solution)/shard_map/all_to_all | solution.py:104
  75.8 10.9 %all-to-all-start = ((bf16[128,2,2048]{2,1,0:T(2,128)(2,1)}), bf16[128,2,2048]{2,1,0:T(2,128)(2,1)S(1)}, u32[]{:S(2)}, u32[]{:S(2)}) async-start(bf16[128,2,2048]{2,1,0:T(2,128)(2,1)} %reshape.450), calls=%async_computation | async-start | bytes 2097152 | tf_op jit(solution)/shard_map/all_to_all | solution.py:103
  87.2 2.2 multiply_reduce_fusion.3
  90.1 4.4 %fusion.21 = (f32[128,1536]{1,0:T(8,128)S(1)}, f32[128,1536]{1,0:T(8,128)S(1)}) fusion(f32[]{:T(128)S(6)} %add.195, bf16[128,1,1536]{2,1,0:T(2,128)(2,1)S(1)} %reshape.453), kind=kLoop, calls=%fused_computation.81 | loop fusion | flops 589824 | bytes 1966084 | tf_op jit(solution)/shard_map/div | solution.py:41
  94.5 1.1 mul.305
  104.3 0.8 convolution_add_fusion.5
  105.6 1.1 dynamic-slice_bitcast_fusion.1
  106.7 9.9 %all-to-all-done = bf16[128,2,2048]{2,1,0:T(2,128)(2,1)S(1)} async-done(((bf16[128,2,2048]{2,1,0:T(2,128)(2,1)}), bf16[128,2,2048]{2,1,0:T(2,128)(2,1)S(1)}, u32[]{:S(2)}, u32[]{:S(2)}) %all-to-all-start) | async-done | bytes 1048608 | tf_op jit(solution)/shard_map/all_to_all | solution.py:103
  116.5 7.0 %all-to-all-start.5 = ((f32[1,128,512]{2,0,1:T(1,128)}), f32[1,128,512]{2,0,1:T(1,128)S(1)}, u32[]{:S(2)}, u32[]{:S(2)}) async-start(f32[1,128,512]{2,0,1:T(1,128)} %dynamic-slice_bitcast_fusion.2), calls=%async_computation.5 | async-start | bytes 524288 | tf_op jit(solution)/shard_map/all_to_all | solution.py:130
  123.6 1.1 reshape.451
  124.7 4.9 %multiply_reduce_fusion.1 = f32[]{:T(128)} fusion(bf16[128,1,4096]{2,1,0:T(2,128)(2,1)S(1)} %reshape.451), kind=kLoop, calls=%fused_computation.16 | loop fusion | flops 1572863 | bytes 1048580 | tf_op jit(solution)/shard_map/reduce_sum | solution.py:40
  130.3 13.6 %fusion.20 = (f32[128,4096]{1,0:T(8,128)}, f32[128,4096]{1,0:T(8,128)}) fusion(f32[]{:T(128)S(6)} %add.181, bf16[128,1,4096]{2,1,0:T(2,128)(2,1)S(1)} %reshape.451), kind=kLoop, calls=%fused_computation.80 | loop fusion | flops 1572864 | bytes 5242884 | tf_op jit(solution)/shard_map/div | solution.py:41
  143.9 2.7 %mul.283 = f32[256,2048]{1,0:T(8,128)} reshape(f32[128,4096]{1,0:T(8,128)} %get-tuple-element.10) | data formatting | bytes 4194304 | tf_op jit(solution)/shard_map/mul | solution.py:58
  146.6 1.9 div.74
  148.5 1.9 fusion.25
  150.8 1.9 convolution_add_fusion.4
  152.7 1.9 fusion.26
  155.0 2.1 convolution_add_fusion.3
  157.1 1.9 fusion.27
  159.4 2.3 convolution_add_fusion.2
  161.6 1.9 fusion.28
  163.9 2.1 convolution_add_fusion.1
  166.0 1.9 fusion.29
  167.9 14.2 %all-to-all-start.3 = ((f32[1,128,768]{2,0,1:T(1,128)}), f32[1,128,768]{2,0,1:T(1,128)S(1)}, u32[]{:S(2)}, u32[]{:S(2)}) async-start(f32[1,128,768]{2,0,1:T(1,128)} %dynamic-slice_bitcast_fusion.1), calls=%async_computation.3 | async-start | bytes 786432 | tf_op jit(solution)/shard_map/all_to_all | solution.py:129
  182.4 3.4 %convolution_add_fusion = f32[256,2048]{1,0:T(8,128)} fusion(f32[256,256]{1,0:T(8,128)S(1)} %fusion, f32[256,2048]{1,0:T(8,128)S(1)} %convolution_add_fusion.1), kind=kOutput, calls=%fused_computation | convolution fusion | flops 1611661312 | bytes 4456448 | tf_op jit(solution)/shard_map/crs,csd->crd/dot_general | solution.py:55
  185.8 2.5 %reshape.431 = f32[1,128,2,2048]{3,2,1,0:T(2,128)S(1)} reshape(f32[256,2048]{1,0:T(8,128)} %convolution_add_fusion) | data formatting | bytes 4194304 | tf_op jit(solution)/shard_map/reshape | solution.py:122
  188.3 2.1 dynamic-slice_bitcast_fusion
  190.4 6.8 %all-to-all-done.3 = f32[1,128,768]{2,0,1:T(1,128)S(1)} async-done(((f32[1,128,768]{2,0,1:T(1,128)}), f32[1,128,768]{2,0,1:T(1,128)S(1)}, u32[]{:S(2)}, u32[]{:S(2)}) %all-to-all-start.3) | async-done | bytes 393248 | tf_op jit(solution)/shard_map/all_to_all | solution.py:129
  197.3 7.0 %all-to-all-start.1 = ((f32[1,128,2048]{2,0,1:T(1,128)}), f32[1,128,2048]{2,0,1:T(1,128)S(1)}, u32[]{:S(2)}, u32[]{:S(2)}) async-start(f32[1,128,2048]{2,0,1:T(1,128)} %dynamic-slice_bitcast_fusion), calls=%async_computation.1 | async-start | bytes 2097152 | tf_op jit(solution)/shard_map/all_to_all | solution.py:128
  206.7 25.8 %all-to-all-done.1 = f32[1,128,2048]{2,0,1:T(1,128)S(1)} async-done(((f32[1,128,2048]{2,0,1:T(1,128)}), f32[1,128,2048]{2,0,1:T(1,128)S(1)}, u32[]{:S(2)}, u32[]{:S(2)}) %all-to-all-start.1) | async-done | bytes 1048608 | tf_op jit(solution)/shard_map/all_to_all | solution.py:128
  233.0 0.9 copy.31
  (76 shorter events, 24.3 us)
Async XLA Ops:
  0.6 22.5 %copy-start.4 = (bf16[48,2048]{1,0:T(8,128)(2,1)S(1)}, bf16[48,2048]{1,0:T(8,128)(2,1)}, u32[]{:S(2)}) copy-start(bf16[48,2048]{1,0:T(8,128)(2,1)} %param.10) | copy-start | bytes 589828
  0.7 22.5 %copy-start.2 = (f32[48,2048]{1,0:T(8,128)S(1)}, f32[48,2048]{1,0:T(8,128)}, u32[]{:S(2)}) copy-start(f32[48,2048]{1,0:T(8,128)} %param.11) | copy-start | bytes 1179652
  8.2 36.9 %all-to-all-start.4 = ((bf16[128,2,512]{2,1,0:T(2,128)(2,1)}), bf16[128,2,512]{2,1,0:T(2,128)(2,1)S(1)}, u32[]{:S(2)}, u32[]{:S(2)}) async-start(bf16[128,2,512]{2,1,0:T(2,128)(2,1)} %reshape.454), calls=%async_computation.4 | async-start | bytes 524288 | tf_op jit(solution)/shard_map/all_to_all | solution.py:105
  28.7 8.7 %copy-start.5 = (bf16[96,768]{1,0:T(8,128)(2,1)S(1)}, bf16[96,768]{1,0:T(8,128)(2,1)}, u32[]{:S(2)}) copy-start(bf16[96,768]{1,0:T(8,128)(2,1)} %param.12) | copy-start | bytes 442372
  35.8 1.6 copy-start.3
  45.1 30.7 %all-to-all-start.2 = ((bf16[128,2,768]{2,1,0:T(2,128)(2,1)}), bf16[128,2,768]{2,1,0:T(2,128)(2,1)S(1)}, u32[]{:S(2)}, u32[]{:S(2)}) async-start(bf16[128,2,768]{2,1,0:T(2,128)(2,1)} %reshape.452), calls=%async_computation.2 | async-start | bytes 786432 | tf_op jit(solution)/shard_map/all_to_all | solution.py:104
  75.8 40.7 %all-to-all-start = ((bf16[128,2,2048]{2,1,0:T(2,128)(2,1)}), bf16[128,2,2048]{2,1,0:T(2,128)(2,1)S(1)}, u32[]{:S(2)}, u32[]{:S(2)}) async-start(bf16[128,2,2048]{2,1,0:T(2,128)(2,1)} %reshape.450), calls=%async_computation | async-start | bytes 2097152 | tf_op jit(solution)/shard_map/all_to_all | solution.py:103
  95.7 1.2 copy-start.1
  116.5 51.3 %all-to-all-start.5 = ((f32[1,128,512]{2,0,1:T(1,128)}), f32[1,128,512]{2,0,1:T(1,128)S(1)}, u32[]{:S(2)}, u32[]{:S(2)}) async-start(f32[1,128,512]{2,0,1:T(1,128)} %dynamic-slice_bitcast_fusion.2), calls=%async_computation.5 | async-start | bytes 524288 | tf_op jit(solution)/shard_map/all_to_all | solution.py:130
  148.5 2.3 copy-start
  167.9 29.4 %all-to-all-start.3 = ((f32[1,128,768]{2,0,1:T(1,128)}), f32[1,128,768]{2,0,1:T(1,128)S(1)}, u32[]{:S(2)}, u32[]{:S(2)}) async-start(f32[1,128,768]{2,0,1:T(1,128)} %dynamic-slice_bitcast_fusion.1), calls=%async_computation.3 | async-start | bytes 786432 | tf_op jit(solution)/shard_map/all_to_all | solution.py:129
  188.3 15.9 %copy-start.6 = (f32[3648]{0:T(1024)S(1)}, f32[3648]{0:T(1024)}, u32[]{:S(2)}) copy-start(f32[3648]{0:T(1024)} %param.16) | copy-start | bytes 43780
  188.3 15.9 %copy-start.7 = (f32[3648]{0:T(1024)S(1)}, f32[3648]{0:T(1024)}, u32[]{:S(2)}) copy-start(f32[3648]{0:T(1024)} %param.18) | copy-start | bytes 43780
  188.3 15.9 %copy-start.8 = (f32[3648]{0:T(1024)S(1)}, f32[3648]{0:T(1024)}, u32[]{:S(2)}) copy-start(f32[3648]{0:T(1024)} %param.19) | copy-start | bytes 43780
  188.3 15.9 %copy-start.9 = (bf16[3648]{0:T(1024)(128)(2,1)S(1)}, bf16[3648]{0:T(1024)(128)(2,1)}, u32[]{:S(2)}) copy-start(bf16[3648]{0:T(1024)(128)(2,1)} %param.17) | copy-start | bytes 21892
  197.3 35.3 %all-to-all-start.1 = ((f32[1,128,2048]{2,0,1:T(1,128)}), f32[1,128,2048]{2,0,1:T(1,128)S(1)}, u32[]{:S(2)}, u32[]{:S(2)}) async-start(f32[1,128,2048]{2,0,1:T(1,128)} %dynamic-slice_bitcast_fusion), calls=%async_computation.1 | async-start | bytes 2097152 | tf_op jit(solution)/shard_map/all_to_all | solution.py:128
where the time goes:
time: 238 us; the launch traced here: 234 us
  starting transfers between devices  67.8 us (28%)
  other arithmetic  46.7 us (20%)
  waiting for transfers between devices  45.5 us (19%)
  matrix products  38.6 us (16%)
  local copies, waits for them, and re-layouts  25.3 us (11%)
  blocking collectives  6.52 us (3%)
  between operations  3.68 us (2%)
    all_to_all x1, waiting for transfers between devices, local(): lax.all_to_all(outgoing[0], 'fsdp', split_axis=1, concat_axis=1, tiled=True)  25.8 us
    div x3, other arithmetic, normalized(): return widened / (frobenius + 1e-07)  21 us
    dot_general x15, matrix products, polish(): jnp.einsum('crs,csd->crd', poly_full, matrices, preferred_element_type=jn...  18.6 us
    dot_general x15, matrix products, gram_terms(): jnp.einsum('crd,csd->crs', matrices, matrices, preferred_element_type=jnp...  16 us
    all_to_all x1, starting transfers between devices, local(): lax.all_to_all(slotted[2], 'fsdp', split_axis=1, concat_axis=1, tiled=True)  15 us
    all_to_all x1, starting transfers between devices, local(): lax.all_to_all(outgoing[1], 'fsdp', split_axis=1, concat_axis=1, tiled=True)  14.2 us
    all_to_all x1, starting transfers between devices, local(): lax.all_to_all(slotted[1], 'fsdp', split_axis=1, concat_axis=1, tiled=True)  13.8 us
    unnamed x3, other arithmetic  12.2 us
  transfers between devices with their start and end apart: 6, of which 4 were waited for; matrix products, arithmetic and copies ran while one was open for 44% of the time, Pallas kernels for 0%

commit v1 on v0

v1 whole, which is shorter than its diff:
```python
import functools
import math

import jax
import jax.numpy as jnp
from jax import lax
from jax.experimental import pallas as pl
from jax.experimental.pallas import tpu as pltpu
from jax.sharding import PartitionSpec as P

MODEL_WIDTH = 2048
LANES = 128
DEVICES = 256
BLOCKS = 16
PER_BLOCK = 16
NS_STEPS = 5
MESH = pl.DeviceIdType.MESH

momentum_rate = 0.95
coef_linear = 3.4445
coef_gram = -4.775
coef_square = 2.0315
bias_first = 1.0 - 0.9**10
bias_second = 1.0 - 0.95**10
highest = lax.Precision.HIGHEST

GATE_SEATS = (0, 6, 12)
RATE_SEATS = (2, 4, 8, 10, 14, 15)
VALUE_SEATS = (3, 5, 9)


def blend_columns(grad_ref, velocity_ref, column):
    piece = pl.ds(column * LANES, LANES)
    widened = grad_ref[:, piece].astype(jnp.float32)
    renewed = momentum_rate * velocity_ref[:, piece] + widened
    return widened + momentum_rate * renewed


def pack_rows(grad_ref, velocity_ref, stage, packed):
    rows, chunks = packed.shape[0], packed.shape[1]
    pitch = 16 if chunks > 8 else 8
    for column in range(chunks):
        stage[pl.ds(column, rows, stride=pitch), :] = blend_columns(
            grad_ref, velocity_ref, column
        )
    staged = stage[pl.ds(0, rows * pitch), :].reshape(rows, pitch, LANES)
    packed[...] = staged[:, :chunks, :].astype(jnp.bfloat16)


def identity(rank):
    row = lax.broadcasted_iota(jnp.int32, (rank, rank), 0)
    column = lax.broadcasted_iota(jnp.int32, (rank, rank), 1)
    return (row == column).astype(jnp.float32)


def product(left, right):
    return jnp.dot(left, right, preferred_element_type=jnp.float32, precision=highest)


def orthogonal_map(raw):
    rank = raw.shape[0]
    eye = identity(rank)
    frobenius = jnp.sqrt(jnp.sum(raw * eye))
    inverse = 1.0 / (frobenius + 1e-07)
    gram = raw * (inverse * inverse)
    total = None
    for iteration in range(NS_STEPS):
        squared = product(gram, gram)
        poly = coef_linear * eye + coef_gram * gram + coef_square * squared
        total = poly if total is None else product(poly, total)
        if iteration < NS_STEPS - 1:
            gram = product(product(poly, gram), poly)
    return total * (inverse * math.sqrt(MODEL_WIDTH))


def split_terms(values):
    first = values.astype(jnp.bfloat16)
    rest = values - first.astype(jnp.float32)
    second = rest.astype(jnp.bfloat16)
    third = (rest - second.astype(jnp.float32)).astype(jnp.bfloat16)
    return first, second, third


def exchange_kernel(
    gate_grad,
    gate_velocity,
    rate_grad,
    rate_velocity,
    value_grad,
    value_velocity,
    gate_back,
    rate_back,
    value_back,
    gate_send,
    rate_send,
    value_send,
    gate_land,
    rate_land,
    value_land,
    stage,
    matrix,
    gate_result,
    rate_result,
    value_result,
    send_sem,
    land_sem,
    result_sem,
    back_sem,
):
    me = lax.axis_index("fsdp") * 2 + lax.axis_index("tp")
    block, seat = me // PER_BLOCK, me % PER_BLOCK

    barrier = pltpu.get_barrier_semaphore()

    def greet(step, carry):
        other = (me + step) % DEVICES
        pl.semaphore_signal(
            barrier, inc=1, device_id=(other // 2, other % 2), device_id_type=MESH
        )
        return carry

    lax.fori_loop(1, DEVICES, greet, 0)

    pack_rows(gate_grad, gate_velocity, stage, gate_send)
    pack_rows(rate_grad, rate_velocity, stage, rate_send)
    pack_rows(value_grad, value_velocity, stage, value_send)

    pl.semaphore_wait(barrier, DEVICES - 1)

    kinds = (
        (GATE_SEATS, gate_send, gate_land, gate_result, gate_back, 0),
        (RATE_SEATS, rate_send, rate_land, rate_result, rate_back, 1),
        (VALUE_SEATS, value_send, value_land, value_result, value_back, 2),
    )

    for seats, send, land, result, back, index in kinds:

        def hand_out(step, carry):
            target = (block + step) % BLOCKS
            for place, offset in enumerate(seats):
                number = target * len(seats) + place
                other = target * PER_BLOCK + offset

                @pl.when(other != me)
                def _():
                    pltpu.make_async_remote_copy(
                        src_ref=send.at[number],
                        dst_ref=land.at[me],
                        send_sem=send_sem.at[index],
                        recv_sem=land_sem.at[index],
                        device_id=(other // 2, other % 2),
                        device_id_type=MESH,
                    ).start()

                @pl.when(other == me)
                def _():
                    pltpu.make_async_copy(
                        send.at[number], land.at[me], land_sem.at[index]
                    ).start()

            return carry

        lax.fori_loop(0, BLOCKS, hand_out, 0)

    def hand_back(number, result, back, index):
        pltpu.make_async_copy(result.at[me], back.at[number], back_sem.at[index]).start()

        def give(step, carry):
            other = (me + step) % DEVICES
            pltpu.make_async_remote_copy(
                src_ref=result.at[other],
                dst_ref=back.at[number],
                send_sem=result_sem.at[0],
                recv_sem=back_sem.at[index],
                device_id=(other // 2, other % 2),
                device_id_type=MESH,
            ).start()
            return carry

        lax.fori_loop(1, DEVICES, give, 0)

    def await_all(ref, sem):
        pltpu.make_async_copy(ref, ref, sem).wait()

    def solve(slabs, land, result, index, number):
        await_all(land, land_sem.at[index])
        chunks = land.shape[1]
        pitch = 16 if chunks > 8 else 8
        rank = sum(count for count, _ in slabs[0])
        view = stage.reshape(stage.shape[0] // pitch, pitch, LANES)
        view[pl.ds(0, DEVICES), pl.ds(0, chunks), :] = land[...].astype(jnp.float32)
        for column, parts in enumerate(slabs):
            row = 0
            for count, (start, stride) in parts:
                matrix[pl.ds(row, count), pl.ds(column * LANES, LANES)] = stage[
                    pl.ds(start, count, stride=stride), :
                ].astype(jnp.bfloat16)
                row += count
        whole = matrix[pl.ds(0, rank), :]
        raw = lax.dot_general(
            whole, whole, (((1,), (1,)), ((), ())), preferred_element_type=jnp.float32
        )
        terms = split_terms(orthogonal_map(raw))
        width = 512
        for start in range(0, MODEL_WIDTH, width):
            piece = matrix[pl.ds(0, rank), pl.ds(start, width)]
            update = sum(
                jnp.dot(term, piece, preferred_element_type=jnp.float32) for term in terms
            )
            for inner in range(width // LANES):
                column = start // LANES + inner
                row = 0
                for count, (offset, stride) in slabs[column]:
                    stage[pl.ds(offset, count, stride=stride), :] = update[
                        row : row + count, inner * LANES : (inner + 1) * LANES
                    ]
                    row += count
        result[...] = view[pl.ds(0, DEVICES), pl.ds(0, chunks), :].astype(jnp.bfloat16)

    gate_slabs = [[(256, (column, 16))] for column in range(16)]
    rate_slabs = []
    for column in range(16):
        parts = []
        for turn in range(3):
            chunk = 16 * turn + column
            parts.append((32, (8 * (chunk // 6) + chunk % 6, 64)))
        rate_slabs.append(parts)
    value_slabs = [
        [(64, (8 * (column // 4) + column % 4, 32))] for column in range(16)
    ]

    is_gate = seat % 6 == 0
    is_value = (seat == 3) | (seat == 5) | (seat == 9)
    is_rate = (
        (seat == 2) | (seat == 4) | (seat == 8) | (seat == 10) | (seat == 14) | (seat == 15)
    )

    @pl.when(is_gate)
    def _():
        number = block * 3 + seat // 6
        solve(gate_slabs, gate_land, gate_result, 0, number)
        hand_back(number, gate_result, gate_back, 0)

    @pl.when(is_rate)
    def _():
        number = block * 6 + (seat + seat // 15 * 3 - 1) // 3
        solve(rate_slabs, rate_land, rate_result, 1, number)
        hand_back(number, rate_result, rate_back, 1)

    @pl.when(is_value)
    def _():
        number = block * 3 + (seat - 1) // 3
        solve(value_slabs, value_land, value_result, 2, number)
        hand_back(number, value_result, value_back, 2)

    def await_sent(ref, sem):
        pltpu.make_async_copy(ref, ref, sem).wait()

    for seats, send, land, result, back, index in kinds:
        await_all(back, back_sem.at[index])

    @pl.when(is_gate)
    def _():
        await_sent(gate_send.at[pl.ds(0, 47)], send_sem.at[0])
        await_sent(gate_result.at[pl.ds(0, 255)], result_sem.at[0])

    @pl.when(jnp.logical_not(is_gate))
    def _():
        await_sent(gate_send, send_sem.at[0])

    @pl.when(is_rate)
    def _():
        await_sent(rate_send.at[pl.ds(0, 95)], send_sem.at[1])
        await_sent(rate_result.at[pl.ds(0, 255)], result_sem.at[0])

    @pl.when(jnp.logical_not(is_rate))
    def _():
        await_sent(rate_send, send_sem.at[1])

    @pl.when(is_value)
    def _():
        await_sent(value_send.at[pl.ds(0, 47)], send_sem.at[2])
        await_sent(value_result.at[pl.ds(0, 255)], result_sem.at[0])

    @pl.when(jnp.logical_not(is_value))
    def _():
        await_sent(value_send, send_sem.at[2])


def unpack_rows(back, stage, out):
    rows, chunks = back.shape[0], back.shape[1]
    pitch = 16 if chunks > 8 else 8
    view = stage.reshape(stage.shape[0] // pitch, pitch, LANES)
    view[pl.ds(0, rows), pl.ds(0, chunks), :] = back[...].astype(jnp.float32)
    for column in range(chunks):
        out[:, pl.ds(column * LANES, LANES)] = stage[pl.ds(column, rows, stride=pitch), :]


def finish_kernel(
    gate_back,
    rate_back,
    value_back,
    gate_grad,
    gate_velocity,
    rate_grad,
    rate_velocity,
    value_grad,
    value_velocity,
    gate_update,
    rate_update,
    value_update,
    gate_renewed,
    rate_renewed,
    value_renewed,
    stage,
):
    for grad, velocity, renewed in (
        (gate_grad, gate_velocity, gate_renewed),
        (rate_grad, rate_velocity, rate_renewed),
        (value_grad, value_velocity, value_renewed),
    ):
        renewed[...] = momentum_rate * velocity[...] + grad[...].astype(jnp.float32)
    unpack_rows(gate_back, stage, gate_update)
    unpack_rows(rate_back, stage, rate_update)
    unpack_rows(value_back, stage, value_update)


def adamw_shard(param_in, grad_in, first_in, second_in):
    widened = grad_in.astype(jnp.float32)
    first_moment_output = 0.9 * first_in + 0.1 * widened
    second_moment_output = 0.95 * second_in + 0.05 * widened * widened
    direction = (
        first_moment_output / bias_first / (jnp.sqrt(second_moment_output / bias_second) + 1e-08)
    )
    parameter_output = param_in - 0.05 * (direction + 0.1 * param_in)
    return (parameter_output, first_moment_output, second_moment_output)


def local(
    gate_gradient,
    gate_velocity,
    rate_factor_gradient,
    rate_factor_velocity,
    value_gradient,
    value_velocity,
    vector_weights,
    vector_gradient,
    vector_first_moment,
    vector_second_moment,
):
    vmem = pl.BlockSpec(memory_space=pltpu.VMEM)
    half, full = jnp.bfloat16, jnp.float32
    packed = ((48, 16, LANES), (96, 6, LANES), (48, 4, LANES))
    landed = tuple((DEVICES,) + shape[1:] for shape in packed)
    factors = (
        gate_gradient,
        gate_velocity,
        rate_factor_gradient,
        rate_factor_velocity,
        value_gradient,
        value_velocity,
    )
    backs = pl.pallas_call(
        exchange_kernel,
        out_shape=[jax.ShapeDtypeStruct(shape, half) for shape in packed],
        in_specs=[vmem] * 6,
        out_specs=[vmem] * 3,
        scratch_shapes=[pltpu.VMEM(shape, half) for shape in packed]
        + [pltpu.VMEM(shape, half) for shape in landed]
        + [
            pltpu.VMEM((DEVICES * 16, LANES), full),
            pltpu.VMEM((256, MODEL_WIDTH), half),
        ]
        + [pltpu.VMEM(shape, half) for shape in landed]
        + [
            pltpu.SemaphoreType.DMA((3,)),
            pltpu.SemaphoreType.DMA((3,)),
            pltpu.SemaphoreType.DMA((1,)),
            pltpu.SemaphoreType.DMA((3,)),
        ],
        compiler_params=pltpu.CompilerParams(collective_id=0, has_side_effects=True),
    )(*factors)
    updates = pl.pallas_call(
        finish_kernel,
        out_shape=[
            jax.ShapeDtypeStruct(array.shape, full)
            for array in (factors[1], factors[3], factors[5]) * 2
        ],
        in_specs=[vmem] * 9,
        out_specs=[vmem] * 6,
        scratch_shapes=[pltpu.VMEM((768, LANES), full)],
    )(*backs, *factors)
    vectors = adamw_shard(
        vector_weights, vector_gradient, vector_first_moment, vector_second_moment
    )
    return (*updates, *vectors)


def solution(mesh):
    split = P(None, ("fsdp", "tp"))
    flat = P(("fsdp", "tp"))
    return jax.shard_map(
        local,
        mesh=mesh,
        in_specs=(split,) * 6 + (flat,) * 4,
        out_specs=(split,) * 6 + (flat,) * 3,
        check_vma=False,
    )
```

time: 238 us -> 60.2 us (0.25)
  the two profiles are of different devices: /device:TPU:32 before, /device:TPU:1 now
where the time goes in v1:
time: 60.2 us; the launch traced here: 60 us
  Pallas kernels  58 us (96%)
  between operations  0.7 us (1%)
  local copies, waits for them, and re-layouts  0.68 us (1%)
  other arithmetic  0.63 us (1%)
    pallas_call x1, Pallas kernels, local(): pl.pallas_call(exchange_kernel, out_shape=[jax.ShapeDtypeStruct(shape, ha...  55.2 us
    pallas_call x1, Pallas kernels, local(): pl.pallas_call(finish_kernel, out_shape=[jax.ShapeDtypeStruct(array.shape...  2.81 us

profile of v1, /device:TPU:1, one launch (start us, length us, event | category | flops | bytes accessed | tf_op | source)
XLA Modules:
  0.0 60.0 jit_solution(18136584794037735740)
XLA Ops:
  0.6 55.2 %shard_map.169 = (bf16[48,16,128]{2,1,0:T(8,128)(2,1)}, bf16[96,6,128]{2,1,0:T(8,128)(2,1)}, bf16[48,4,128]{2,1,0:T(4,128)(2,1)}) custom-call(bf16[48,2048]{1,0:T(8,128)(2,1)} %gate_grad.3, f32[48,2048]{1,0:T(8,128)} %gate_velocity.3, bf16[96,768]{1,0:T(8,128)(2,1)} %rate_grad.3, f32[96,768]{1,0:T(8,128)} %rate_velocity.3, bf16[48,512]{1,0:T(8,128)(2,1)} %value_grad.3, ...), custom_call_target="tpu_custom_call" | custom-call | tf_op jit(solution)/shard_map/pallas_call | solution.py:363
  55.8 0.0 copy-start
  55.9 0.0 copy-start.1
  55.9 0.0 copy-start.2
  55.9 2.8 %shard_map.170 = (f32[48,2048]{1,0:T(8,128)}, f32[96,768]{1,0:T(8,128)}, f32[48,512]{1,0:T(8,128)}, f32[48,2048]{1,0:T(8,128)}, f32[96,768]{1,0:T(8,128)}, /*index=5*/f32[48,512]{1,0:T(8,128)}) custom-call(bf16[48,16,128]{2,1,0:T(8,128)(2,1)} %get-tuple-element.18.gate_back, bf16[96,6,128]{2,1,0:T(8,128)(2,1)} %get-tuple-element.19.rate_back, ...), custom_call_target="tpu_custom_call" | custom-call | tf_op jit(solution)/shard_map/pallas_call | solution.py:383
  58.7 0.0 copy-start.3
  58.7 0.0 copy-done
  58.7 0.0 copy-done.1
  58.7 0.0 copy-done.2
  58.7 0.7 %copy-done.3 = bf16[3648]{0:T(1024)(128)(2,1)S(1)} copy-done((bf16[3648]{0:T(1024)(128)(2,1)S(1)}, bf16[3648]{0:T(1024)(128)(2,1)}, u32[]{:S(2)}) %copy-start.3) | copy-done | bytes 7320
  59.4 0.6 %multiply_subtract_fusion = (f32[3648]{0:T(1024)}, f32[3648]{0:T(1024)}, f32[3648]{0:T(1024)}) fusion(f32[3648]{0:T(1024)S(1)} %copy-done, bf16[3648]{0:T(1024)(128)(2,1)S(1)} %copy-done.3, f32[3648]{0:T(1024)S(1)} %copy-done.1, f32[3648]{0:T(1024)S(1)} %copy-done.2), kind=kLoop, calls=%fused_computation.4 | loop fusion | flops 58368 | bytes 94848 | tf_op jit(solution)/shard_map/sub | solution.py:335
Async XLA Ops:
  55.8 2.9 %copy-start = (f32[3648]{0:T(1024)S(1)}, f32[3648]{0:T(1024)}, u32[]{:S(2)}) copy-start(f32[3648]{0:T(1024)} %param.16) | copy-start | bytes 43780
  55.9 2.9 %copy-start.1 = (f32[3648]{0:T(1024)S(1)}, f32[3648]{0:T(1024)}, u32[]{:S(2)}) copy-start(f32[3648]{0:T(1024)} %param.18) | copy-start | bytes 43780
  55.9 2.9 %copy-start.2 = (f32[3648]{0:T(1024)S(1)}, f32[3648]{0:T(1024)}, u32[]{:S(2)}) copy-start(f32[3648]{0:T(1024)} %param.19) | copy-start | bytes 43780
  58.7 0.7 %copy-start.3 = (bf16[3648]{0:T(1024)(128)(2,1)S(1)}, bf16[3648]{0:T(1024)(128)(2,1)}, u32[]{:S(2)}) copy-start(bf16[3648]{0:T(1024)(128)(2,1)} %param.17) | copy-start | bytes 21892

commit v2 on v1

--- a/solution.py
+++ b/solution.py
@@ -22,7 +22,6 @@
 coef_square = 2.0315
 bias_first = 1.0 - 0.9**10
 bias_second = 1.0 - 0.95**10
-highest = lax.Precision.HIGHEST
 
 GATE_SEATS = (0, 6, 12)
 RATE_SEATS = (2, 4, 8, 10, 14, 15)
@@ -53,8 +52,18 @@
     return (row == column).astype(jnp.float32)
 
 
+def split_terms(values):
+    first = values.astype(jnp.bfloat16)
+    second = (values - first.astype(jnp.float32)).astype(jnp.bfloat16)
+    return first, second
+
+
 def product(left, right):
-    return jnp.dot(left, right, preferred_element_type=jnp.float32, precision=highest)
+    def multiply(x, y):
+        return jnp.dot(x, y, preferred_element_type=jnp.float32)
+
+    (high, low), (top, rest) = left, right
+    return multiply(high, top) + (multiply(high, rest) + multiply(low, top))
 
 
 def orthogonal_map(raw):
@@ -65,20 +74,14 @@
     gram = raw * (inverse * inverse)
     total = None
     for iteration in range(NS_STEPS):
-        squared = product(gram, gram)
+        gram_terms = split_terms(gram)
+        squared = product(gram_terms, gram_terms)
         poly = coef_linear * eye + coef_gram * gram + coef_square * squared
-        total = poly if total is None else product(poly, total)
+        poly_terms = split_terms(poly)
+        total = poly if total is None else product(poly_terms, split_terms(total))
         if iteration < NS_STEPS - 1:
-            gram = product(product(poly, gram), poly)
+            gram = product(split_terms(product(poly_terms, gram_terms)), poly_terms)
     return total * (inverse * math.sqrt(MODEL_WIDTH))
-
-
-def split_terms(values):
-    first = values.astype(jnp.bfloat16)
-    rest = values - first.astype(jnp.float32)
-    second = rest.astype(jnp.bfloat16)
-    third = (rest - second.astype(jnp.float32)).astype(jnp.bfloat16)
-    return first, second, third
 
 
 def exchange_kernel(

time: 60.2 us -> 58.5 us (0.972)
  Pallas kernels: 58 us -> 56.3 us
    pallas_call x1, Pallas kernels: 55.2 us -> 53.5 us  [local(): pl.pallas_call(exchange_kernel, out_shape=[jax.ShapeDtypeStruct(shape, ha...]
where the time goes in v2:
time: 58.5 us; the launch traced here: 58.3 us
  Pallas kernels  56.3 us (96%)
  between operations  0.7 us (1%)
  local copies, waits for them, and re-layouts  0.68 us (1%)
  other arithmetic  0.63 us (1%)
    pallas_call x1, Pallas kernels, local(): pl.pallas_call(exchange_kernel, out_shape=[jax.ShapeDtypeStruct(shape, ha...  53.5 us
    pallas_call x1, Pallas kernels, local(): pl.pallas_call(finish_kernel, out_shape=[jax.ShapeDtypeStruct(array.shape...  2.81 us

profile of v2, /device:TPU:1, one launch (start us, length us, event | category | flops | bytes accessed | tf_op | source)
XLA Modules:
  0.0 58.3 jit_solution(1955343494500504366)
XLA Ops:
  0.6 53.5 %shard_map.169 = (bf16[48,16,128]{2,1,0:T(8,128)(2,1)}, bf16[96,6,128]{2,1,0:T(8,128)(2,1)}, bf16[48,4,128]{2,1,0:T(4,128)(2,1)}) custom-call(bf16[48,2048]{1,0:T(8,128)(2,1)} %gate_grad.3, f32[48,2048]{1,0:T(8,128)} %gate_velocity.3, bf16[96,768]{1,0:T(8,128)(2,1)} %rate_grad.3, f32[96,768]{1,0:T(8,128)} %rate_velocity.3, bf16[48,512]{1,0:T(8,128)(2,1)} %value_grad.3, ...), custom_call_target="tpu_custom_call" | custom-call | tf_op jit(solution)/shard_map/pallas_call | solution.py:366
  54.1 0.0 copy-start
  54.1 0.0 copy-start.1
  54.1 0.0 copy-start.2
  54.1 2.8 %shard_map.170 = (f32[48,2048]{1,0:T(8,128)}, f32[96,768]{1,0:T(8,128)}, f32[48,512]{1,0:T(8,128)}, f32[48,2048]{1,0:T(8,128)}, f32[96,768]{1,0:T(8,128)}, /*index=5*/f32[48,512]{1,0:T(8,128)}) custom-call(bf16[48,16,128]{2,1,0:T(8,128)(2,1)} %get-tuple-element.18.gate_back, bf16[96,6,128]{2,1,0:T(8,128)(2,1)} %get-tuple-element.19.rate_back, ...), custom_call_target="tpu_custom_call" | custom-call | tf_op jit(solution)/shard_map/pallas_call | solution.py:386
  57.0 0.0 copy-start.3
  57.0 0.0 copy-done
  57.0 0.0 copy-done.1
  57.0 0.0 copy-done.2
  57.0 0.7 %copy-done.3 = bf16[3648]{0:T(1024)(128)(2,1)S(1)} copy-done((bf16[3648]{0:T(1024)(128)(2,1)S(1)}, bf16[3648]{0:T(1024)(128)(2,1)}, u32[]{:S(2)}) %copy-start.3) | copy-done | bytes 7320
  57.7 0.6 %multiply_subtract_fusion = (f32[3648]{0:T(1024)}, f32[3648]{0:T(1024)}, f32[3648]{0:T(1024)}) fusion(f32[3648]{0:T(1024)S(1)} %copy-done, bf16[3648]{0:T(1024)(128)(2,1)S(1)} %copy-done.3, f32[3648]{0:T(1024)S(1)} %copy-done.1, f32[3648]{0:T(1024)S(1)} %copy-done.2), kind=kLoop, calls=%fused_computation.4 | loop fusion | flops 58368 | bytes 94848 | tf_op jit(solution)/shard_map/sub | solution.py:338
Async XLA Ops:
  54.1 2.9 %copy-start = (f32[3648]{0:T(1024)S(1)}, f32[3648]{0:T(1024)}, u32[]{:S(2)}) copy-start(f32[3648]{0:T(1024)} %param.16) | copy-start | bytes 43780
  54.1 2.9 %copy-start.1 = (f32[3648]{0:T(1024)S(1)}, f32[3648]{0:T(1024)}, u32[]{:S(2)}) copy-start(f32[3648]{0:T(1024)} %param.18) | copy-start | bytes 43780
  54.1 2.9 %copy-start.2 = (f32[3648]{0:T(1024)S(1)}, f32[3648]{0:T(1024)}, u32[]{:S(2)}) copy-start(f32[3648]{0:T(1024)} %param.19) | copy-start | bytes 43780
  57.0 0.7 %copy-start.3 = (bf16[3648]{0:T(1024)(128)(2,1)S(1)}, bf16[3648]{0:T(1024)(128)(2,1)}, u32[]{:S(2)}) copy-start(bf16[3648]{0:T(1024)(128)(2,1)} %param.17) | copy-start | bytes 21892
